TPU v7x, 256 devices: a whole 4x4x8 slice. The times are simulated.
256 devices in a mesh: tm: 32 (over x, z), chan: 8 (over y, core).
Axes of the slice: x: 4, y: 4, z: 8, core: 2. Of those that a mesh axis runs over, the one named last changes fastest.
Arguments:
- visibilities: bfloat16 [32, 8, 512, 1024], P('tm', None, None, 'chan'), may hold values from -6 to 6
- station_gains: float32 [8, 192, 1024], P(None, 'chan'), may hold values from -1.5 to 1.5, as said below
- station_pairs: int32 [512, 2], replicated, may hold values from 0 to 191, as said below
- average_bands: int32 [512, 2], replicated, may hold values from 0 to 3, as said below
- tile_map: int32 [512, 32], replicated, may hold values from 0 to 255
- baseline_order: int32 [512], replicated, may hold values from 0 to 511, as said below
Outputs:
- averaged: bfloat16 [32, 8, 512, 1024], P(None, None, 'tm', 'chan')
- gridded: float32 [256, 8, 1024], P('tm', None, 'chan')
Inputs may be any that keep to these rules, and one draw needn't show every extreme that they name: `station_pairs`: row b holds the two stations of baseline b, the first smaller than the second. `average_bands`: column 0 is at most 3, column 1 at most 2. In each aligned block of 16 positions k of baseline_order, the bands of the baselines baseline_order[k] are, in some order, the pairs (3 - j % (3 + 1), 2 - j % (2 + 1)) for j = 0 to 15. `baseline_order`: each baseline once. `station_gains`: diagonal Jones entries have magnitudes of order one.
All inputs are finite; a program needn't handle non-finite values.
Results may differ from a plain program's by a relative error of at most 0.019.
Values may be sent and summed in bfloat16 or wider, within the bound.
No kernel may reach another device: no remote copies, remote signals or barrier semaphores. Data moves between devices by JAX's collectives and lax.ppermute only.
A program may use at most 128 MiB of HBM per device.

v0:
```python
import jax
import jax.numpy as jnp
from jax import lax
from jax.sharding import PartitionSpec as P

TILE_DEV = 8
TLOG = 3
CLOG = 2


def product(left, right):
    return (left[0] * right[0] - left[1] * right[1], left[0] * right[1] + left[1] * right[0])


def product_conj(left, right):
    return (left[0] * right[0] + left[1] * right[1], left[1] * right[0] - left[0] * right[1])


def add_pair(left, right):
    return (left[0] + right[0], left[1] + right[1])


def as_matrix(components):
    return [
        [(components[0], components[1]), (components[2], components[3])],
        [(components[4], components[5]), (components[6], components[7])],
    ]


def jones_apply(first, middle, second):
    left_gain = as_matrix(first)
    coherency = as_matrix(middle)
    right_gain = as_matrix(second)
    partial_rows = [
        [
            add_pair(
                product(left_gain[i][0], coherency[0][k]), product(left_gain[i][1], coherency[1][k])
            )
            for k in range(2)
        ]
        for i in range(2)
    ]
    result = []
    for i in range(2):
        for c in range(2):
            element = add_pair(
                product_conj(partial_rows[i][0], right_gain[c][0]),
                product_conj(partial_rows[i][1], right_gain[c][1]),
            )
            result.extend(element)
    return result


def calibrate(samples, gain_table, first_station, second_station):
    left_gain = jnp.take(gain_table, first_station, axis=1)
    right_gain = jnp.take(gain_table, second_station, axis=1)
    values = [samples[:, i].astype(jnp.float32) for i in range(8)]
    result = jones_apply(
        [left_gain[i][None] for i in range(8)], values, [right_gain[i][None] for i in range(8)]
    )
    return jnp.stack(result, axis=1).astype(jnp.bfloat16)


def halve_time(current, size):
    extent = current.shape[0]
    shaped = current.reshape((extent // size, 2, size // 2) + current.shape[1:])
    merged = 0.5 * (shaped[:, 0:1] + shaped[:, 1:2])
    return jnp.broadcast_to(merged, shaped.shape).reshape(current.shape)


def halve_chan(current, size):
    extent = current.shape[-1]
    shaped = current.reshape(current.shape[:-1] + (extent // size, 2, size // 2))
    merged = 0.5 * (shaped[..., 0:1, :] + shaped[..., 1:2, :])
    return jnp.broadcast_to(merged, shaped.shape).reshape(current.shape)


def band_average(samples, time_levels, chan_levels):
    values = samples.astype(jnp.float32)
    time_select = time_levels[None, None, :, None]
    chan_select = chan_levels[None, None, :, None]
    result = values
    current = values
    for k in range(1, TLOG + 1):
        current = halve_time(current, 2**k)
        result = jnp.where(time_select >= k, current, result)
    final = result
    current = result
    for k in range(1, CLOG + 1):
        current = halve_chan(current, 2**k)
        final = jnp.where(chan_select >= k, current, final)
    return final.astype(jnp.bfloat16)


def shards(visibilities, station_gains, station_pairs, average_bands, tile_map, baseline_order):
    chan_width = visibilities.shape[3]
    block_size = visibilities.shape[2] // lax.axis_size("tm")
    all_gains = lax.all_gather(station_gains, "chan", axis=1, tiled=True)
    gain_table = lax.dynamic_slice_in_dim(
        all_gains, lax.axis_index("chan") * chan_width, chan_width, 2
    )
    reordered = jnp.take(visibilities, baseline_order, axis=2)
    rows_here = lax.dynamic_slice_in_dim(
        baseline_order, lax.axis_index("tm") * block_size, block_size
    )
    bands_here = average_bands[rows_here]
    ordered_pairs = station_pairs[baseline_order]
    payload = calibrate(reordered, gain_table, ordered_pairs[:, 0], ordered_pairs[:, 1])
    turned = lax.all_to_all(payload, "tm", split_axis=2, concat_axis=0, tiled=True)
    averaged = band_average(turned, bands_here[:, 0], bands_here[:, 1])
    tile_here = tile_map[rows_here].T
    time_index = jnp.arange(averaged.shape[0], dtype=jnp.int32)[:, None]
    period = jnp.left_shift(jnp.ones_like(bands_here[:, 0]), bands_here[:, 0])[None, :]
    tile_ids = jnp.where(time_index % period == 0, tile_here, -1)
    targets = jnp.arange(TILE_DEV * lax.axis_size("tm"), dtype=jnp.int32)
    one_hot = (tile_ids[None] == targets[:, None, None]).astype(jnp.bfloat16)
    gridded = lax.psum_scatter(
        jnp.einsum("rtb,tkbc->rkc", one_hot, averaged, preferred_element_type=jnp.float32).astype(
            jnp.bfloat16
        ),
        "tm",
        scatter_dimension=0,
        tiled=True,
    ).astype(jnp.float32)
    return (averaged, gridded)


def solution(mesh):
    return jax.shard_map(
        shards,
        mesh=mesh,
        in_specs=(P("tm", None, None, "chan"), P(None, "chan", None), P(), P(), P(), P()),
        out_specs=(P(None, None, "tm", "chan"), P("tm", None, "chan")),
        check_vma=False,
    )
```

profile of v0, /device:TPU:8, one launch (start us, length us, event | category | flops | bytes accessed | tf_op | source)
XLA Modules:
  0.0 475.1 jit_solution(13990417689148985308)
XLA Ops:
  7.2 2.5 copy.586
  10.0 0.7 copy.639
  10.7 1.0 gather_fusion.1
  11.8 1.8 gather_fusion.2
  14.1 41.8 %all-gather.2.cloned.1.call-done = f32[8,192,1024]{2,0,1:T(8,128)} async-done(((f32[8,24,1024]{2,0,1:T(8,128)}), f32[8,192,1024]{2,0,1:T(8,128)}) %all-gather.2.cloned.1.call-update) | async-done | bytes 6291472 | tf_op jit(solution)/shard_map/all_gather | solution.py:98
  55.9 1.2 constant_dynamic-slice_fusion
  57.1 2.7 gather_fusion.5
  59.8 2.7 gather_fusion.4
  62.5 2.2 fusion.11
  66.8 1.6 copy.591
  68.5 9.8 %all-to-all-start = ((bf16[1,8,512,128]{3,1,0,2:T(8,128)(2,1)}), bf16[1,8,512,128]{3,1,0,2:T(8,128)(2,1)S(1)}, u32[]{:S(2)}, u32[]{:S(2)}) async-start(bf16[1,8,512,128]{3,1,0,2:T(8,128)(2,1)} %copy.591), calls=%async_computation | async-start | bytes 2097152 | tf_op jit(solution)/shard_map/all_to_all | solution.py:109
  79.3 0.6 gather_fusion.3
  80.0 0.8 compare_reduce_fusion.4
  81.0 26.3 %all-to-all-done = bf16[1,8,512,128]{3,1,0,2:T(8,128)(2,1)S(1)} async-done(((bf16[1,8,512,128]{3,1,0,2:T(8,128)(2,1)}), bf16[1,8,512,128]{3,1,0,2:T(8,128)(2,1)S(1)}, u32[]{:S(2)}, u32[]{:S(2)}) %all-to-all-start) | async-done | bytes 1048608 | tf_op jit(solution)/shard_map/all_to_all | solution.py:109
  107.4 1.6 convert_bitcast_fusion
  109.2 1.1 fusion.59
  110.6 2.8 copy.621
  113.3 2.6 copy.620
  116.0 5.8 %add_multiply_fusion = f32[8,1,8,16,128]{3,2,4,0,1:T(8,128)} fusion(f32[8,1,8,16,128]{3,2,4,0,1:T(8,128)} %copy.620, f32[8,1,8,16,128]{3,2,4,0,1:T(8,128)} %copy.621), kind=kLoop, calls=%fused_computation.7 | loop fusion | flops 262144 | bytes 1572864 | tf_op jit(solution)/shard_map/mul | solution.py:67
  121.8 2.7 copy.625
  124.5 2.4 fusion.5
  126.9 0.6 copy.624
  127.6 6.6 %copy.598 = f32[32,1,8,16,128]{0,3,4,2,1:T(8,128)} copy(f32[32,1,8,16,128]{4,3,0,2,1:T(8,128)} %convert_bitcast_fusion) | data formatting | bytes 4194304 | tf_op jit(solution)/shard_map/convert_element_type | solution.py:79
  134.2 8.7 %copy.600 = f32[32,8,16,64,2,1]{3,2,5,4,1,0:T(8,128)} copy(f32[32,8,16,64,2,1]{0,2,4,3,1,5:T(8,128)} %bitcast.225) | data formatting | bytes 4194304 | tf_op jit(solution)/shard_map/convert_element_type | solution.py:79
  142.9 6.0 %copy.597 = f32[16,8,16,128]{2,1,3,0:T(8,128)} copy(f32[16,8,16,128]{3,2,0,1:T(8,128)} %fusion.59) | data formatting | bytes 2097152 | tf_op jit(solution)/shard_map/broadcast_in_dim | solution.py:68
  148.9 11.0 %broadcast_in_dim.122 = f32[16,2,8,16,128]{3,2,4,1,0:T(8,128)} broadcast(f32[16,8,16,128]{2,1,3,0:T(8,128)} %copy.597), dimensions={0,2,3,4} | broadcast | bytes 3145728 | tf_op jit(solution)/shard_map/broadcast_in_dim | solution.py:68
  159.9 11.9 %copy.599 = f32[32,8,16,64,2,1]{3,2,5,4,1,0:T(8,128)} copy(f32[32,8,16,64,2,1]{2,1,4,3,0,5:T(8,128)} %bitcast.219) | data formatting | bytes 4194304 | tf_op jit(solution)/shard_map/broadcast_in_dim | solution.py:68
  171.8 7.6 %broadcast_in_dim.117 = f32[4,2,4,8,16,128]{4,3,5,2,1,0:T(8,128)} broadcast(f32[4,8,16,128]{2,1,3,0:T(8,128)S(1)} %fusion.5), dimensions={0,3,4,5} | broadcast | bytes 2359296 | tf_op jit(solution)/shard_map/broadcast_in_dim | solution.py:68
  179.4 12.0 %copy.602 = f32[32,8,16,64,2,1]{3,2,5,4,1,0:T(8,128)} copy(f32[32,8,16,64,2,1]{2,1,4,3,0,5:T(8,128)} %bitcast.220) | data formatting | bytes 4194304 | tf_op jit(solution)/shard_map/reshape | solution.py:68
  191.4 10.2 %broadcast_in_dim.119 = f32[8,2,2,8,16,128]{4,3,5,2,1,0:T(8,128)} broadcast(f32[8,8,16,128]{2,1,3,0:T(8,128)} %bitcast.224), dimensions={0,3,4,5} | broadcast | bytes 2621440 | tf_op jit(solution)/shard_map/broadcast_in_dim | solution.py:68
  201.6 11.9 %copy.601 = f32[32,8,16,64,2,1]{3,2,5,4,1,0:T(8,128)} copy(f32[32,8,16,64,2,1]{2,1,4,3,0,5:T(8,128)} %bitcast.221) | data formatting | bytes 4194304 | tf_op jit(solution)/shard_map/reshape | solution.py:68
  213.5 8.0 %select_select_fusion = f32[32,8,16,64,2,1]{3,2,5,4,1,0:T(8,128)S(1)} fusion(f32[32,8,16,64,2,1]{3,2,5,4,1,0:T(8,128)} %copy.602, f32[32,8,16,64,2,1]{3,2,5,4,1,0:T(8,128)} %copy.601, f32[32,8,16,64,2,1]{3,2,5,4,1,0:T(8,128)} %copy.599, f32[32,8,16,64,2,1]{3,2,5,4,1,0:T(8,128)} %copy.600, pred[16]{0:T(512)(128)(4,1)S(1)} %get-tuple-element.31, ...), kind=kLoop, calls=%fused_computation.6 | loop fusion | flops 1572864 | bytes 10485808 | tf_op jit(solution)/shard_map/jit(_where)/select_n | solution.py:86
  221.6 1.7 fusion.58
  223.6 4.5 copy.606
  228.2 4.1 broadcast_in_dim.128
  232.3 6.1 %copy.610 = bf16[32,8,16,128]{3,2,0,1:T(8,128)(2,1)} copy(bf16[32,8,16,128]{0,2,3,1:T(8,128)(2,1)} %bitcast.228) | data formatting | bytes 2097152 | tf_op jit(solution)/shard_map/broadcast_in_dim | solution.py:75
  238.4 3.6 copy.603
  242.0 2.5 fusion.1
  244.5 2.5 broadcast_in_dim.125
  247.0 6.2 %copy.611 = bf16[32,8,16,128]{3,2,0,1:T(8,128)(2,1)} copy(bf16[32,8,16,128]{0,2,3,1:T(8,128)(2,1)} %bitcast.230) | data formatting | bytes 2097152 | tf_op jit(solution)/shard_map/reshape | solution.py:75
  253.7 0.8 copy-done.2
  254.8 1.0 fusion.10
  255.7 0.6 fusion.14
  256.3 0.9 copy.640
  257.3 1.3 copy.614
  258.5 208.4 %reduce-scatter.4.cloned.1.call-done = bf16[8,1024]{1,0:T(8,128)(2,1)} async-done(((bf16[256,1024]{1,0:T(8,128)(2,1)}), bf16[8,1024]{1,0:T(8,128)(2,1)}) %reduce-scatter.4.cloned.1.call-update) | async-done | bytes 16400
  466.9 0.7 bitcast_convert_fusion
  467.6 0.6 copy.615
  (65 shorter events, 5.8 us)
Async XLA Ops:
  7.2 2.7 copy-start.9
  7.2 2.8 copy-start.4
  7.2 3.5 copy-start.6
  7.2 48.7 %all-gather.2.cloned.1.call-start = ((), (), s32[]{:S(2)}) async-start(), calls=%async_computation.2 | async-start | bytes 7077888 | tf_op jit(solution)/shard_map/all_gather | solution.py:98
  62.5 2.2 copy-start.1
  66.8 11.6 %copy-start.10 = (s32[512,2]{0,1:T(2,128)S(1)}, s32[512,2]{0,1:T(2,128)}, u32[]{:S(2)}) copy-start(s32[512,2]{0,1:T(2,128)} %param.11) | copy-start | bytes 12292
  66.8 11.7 %copy-start.5 = (s32[512,32]{0,1:T(8,128)S(1)}, s32[512,32]{0,1:T(8,128)}, u32[]{:S(2)}) copy-start(s32[512,32]{0,1:T(8,128)} %param.12) | copy-start | bytes 196612
  68.5 38.8 %all-to-all-start = ((bf16[1,8,512,128]{3,1,0,2:T(8,128)(2,1)}), bf16[1,8,512,128]{3,1,0,2:T(8,128)(2,1)S(1)}, u32[]{:S(2)}, u32[]{:S(2)}) async-start(bf16[1,8,512,128]{3,1,0,2:T(8,128)(2,1)} %copy.591), calls=%async_computation | async-start | bytes 2097152 | tf_op jit(solution)/shard_map/all_to_all | solution.py:109
  78.3 388.6 %reduce-scatter.4.cloned.1.call-start = ((), (), s32[]{:S(2)}) async-start(), calls=%async_computation.3 | async-start | bytes 540672
  201.6 11.9 %copy-start.7 = (pred[16]{0:T(512)(128)(4,1)S(1)}, pred[16]{0:T(512)(128)(4,1)}, u32[]{:S(2)}) copy-start(pred[16]{0:T(512)(128)(4,1)} %get-tuple-element.33) | copy-start | bytes 52
  247.0 6.2 %copy-start = (f32[16,8,16,128]{3,2,0,1:T(8,128)S(1)}, f32[16,8,16,128]{3,2,0,1:T(8,128)}, u32[]{:S(2)}) copy-start(f32[16,8,16,128]{3,2,0,1:T(8,128)} %fusion.59) | copy-start | bytes 3145732
  253.2 1.2 copy-start.2
  253.2 1.5 copy-start.3
  253.2 1.5 copy-start.8
  253.2 1.5 copy-start.11
  253.2 1.5 copy-start.12
Sparse Core Ops, SparseCore 0:
  10.4 45.4 all-gather.1
  257.4 209.4 reduce-scatter.3
where the time goes:
time: 476 us; the launch traced here: 475 us
  waiting for transfers between devices  276 us (58%)
  local copies, waits for them, and re-layouts  142 us (30%)
  other arithmetic  31.2 us (7%)
  between operations  14.4 us (3%)
  starting transfers between devices  9.9 us (2%)
    unnamed x3, waiting for transfers between devices  208 us
    broadcast_in_dim x8, local copies, waits for them, and re-layouts, halve_time(): return jnp.broadcast_to(merged, shaped.shape).reshape(current.shape)  47.1 us
    all_gather x1, waiting for transfers between devices, shards(): all_gains = lax.all_gather(station_gains, 'chan', axis=1, tiled=True)  41.8 us
    all_to_all x1, waiting for transfers between devices, shards(): lax.all_to_all(payload, 'tm', split_axis=2, concat_axis=0, tiled=True)  26.3 us
    reshape x2, local copies, waits for them, and re-layouts, halve_time(): return jnp.broadcast_to(merged, shaped.shape).reshape(current.shape)  23.9 us
    broadcast_in_dim x4, local copies, waits for them, and re-layouts, halve_chan(): return jnp.broadcast_to(merged, shaped.shape).reshape(current.shape)  17.2 us
    unnamed x38, local copies, waits for them, and re-layouts  16.4 us
    convert_element_type x2, local copies, waits for them, and re-layouts, band_average(): values = samples.astype(jnp.float32)  15.3 us
  transfers between devices with their start and end apart: 3, of which 3 were waited for; matrix products, arithmetic and copies ran while one was open for 2% of the time, Pallas kernels for 0%

commit v1 on v0

--- a/solution.py
+++ b/solution.py
@@ -1,3 +1,4 @@
+import functools
 import jax
 import jax.numpy as jnp
 from jax import lax
@@ -6,6 +7,15 @@
 TILE_DEV = 8
 TLOG = 3
 CLOG = 2
+
+
+def deliver_domain_on(local, link_axis, axis_no, row_dim):
+    state_next = jnp.stack(jnp.split(local, lax.axis_size(link_axis), axis_no), 0)
+    e_now = jnp.concatenate(lax.all_to_all(state_next, link_axis, 0, 0), row_dim)
+    return e_now
+
+
+write_the_panel = functools.partial(deliver_domain_on, link_axis="tm", axis_no=2, row_dim=0)
 
 
 def product(left, right):
@@ -106,7 +116,7 @@
     bands_here = average_bands[rows_here]
     ordered_pairs = station_pairs[baseline_order]
     payload = calibrate(reordered, gain_table, ordered_pairs[:, 0], ordered_pairs[:, 1])
-    turned = lax.all_to_all(payload, "tm", split_axis=2, concat_axis=0, tiled=True)
+    turned = write_the_panel(payload)
     averaged = band_average(turned, bands_here[:, 0], bands_here[:, 1])
     tile_here = tile_map[rows_here].T
     time_index = jnp.arange(averaged.shape[0], dtype=jnp.int32)[:, None]

time: 476 us -> 491 us (1.032)
  local copies, waits for them, and re-layouts: 142 us -> 157 us
    unnamed x38 -> x62, local copies, waits for them, and re-layouts: 16.4 us -> 32.9 us
    broadcast_in_dim x8 -> x5, local copies, waits for them, and re-layouts: 47.1 us -> 46.7 us  [halve_time(): return jnp.broadcast_to(merged, shaped.shape).reshape(current.shape)]
  transfers between devices with their start and end apart: 3 -> 3, of which waited for: 3 -> 3; matrix products, arithmetic and copies ran while one was open for 2% -> 1% of each run, Pallas kernels for 0% -> 0%
where the time goes in v1:
time: 491 us; the launch traced here: 490 us
  waiting for transfers between devices  277 us (56%)
  local copies, waits for them, and re-layouts  157 us (32%)
  other arithmetic  30.8 us (6%)
  between operations  14.4 us (3%)
  starting transfers between devices  10.1 us (2%)
    unnamed x3, waiting for transfers between devices  209 us
    broadcast_in_dim x5, local copies, waits for them, and re-layouts, halve_time(): return jnp.broadcast_to(merged, shaped.shape).reshape(current.shape)  46.7 us
    all_gather x1, waiting for transfers between devices, shards(): all_gains = lax.all_gather(station_gains, 'chan', axis=1, tiled=True)  41.8 us
    unnamed x62, local copies, waits for them, and re-layouts  32.9 us
    all_to_all x1, waiting for transfers between devices, deliver_domain_on(): lax.all_to_all(state_next, link_axis, 0, 0)  26.1 us
    reshape x2, local copies, waits for them, and re-layouts, halve_time(): return jnp.broadcast_to(merged, shaped.shape).reshape(current.shape)  23.9 us
    broadcast_in_dim x4, local copies, waits for them, and re-layouts, halve_chan(): return jnp.broadcast_to(merged, shaped.shape).reshape(current.shape)  17.5 us
    convert_element_type x2, local copies, waits for them, and re-layouts, band_average(): values = samples.astype(jnp.float32)  13.8 us
  transfers between devices with their start and end apart: 3, of which 3 were waited for; matrix products, arithmetic and copies ran while one was open for 1% of the time, Pallas kernels for 0%

profile of v1, /device:TPU:8, one launch (start us, length us, event | category | flops | bytes accessed | tf_op | source)
XLA Modules:
  0.0 489.9 jit_solution(18378595434833308072)
XLA Ops:
  7.2 2.5 copy.605
  10.0 0.7 copy.655
  10.7 1.0 gather_fusion.1
  11.8 1.8 gather_fusion.2
  14.1 41.8 %all-gather.2.cloned.1.call-done = f32[8,192,1024]{2,0,1:T(8,128)} async-done(((f32[8,24,1024]{2,0,1:T(8,128)}), f32[8,192,1024]{2,0,1:T(8,128)}) %all-gather.2.cloned.1.call-update) | async-done | bytes 6291472 | tf_op jit(solution)/shard_map/all_gather | solution.py:108
  55.9 1.2 constant_dynamic-slice_fusion
  57.1 2.7 gather_fusion.5
  59.9 2.7 gather_fusion.4
  62.5 2.2 fusion.11
  66.8 0.6 constant_dynamic-update-slice_fusion.31
  68.7 0.6 constant_dynamic-update-slice_fusion.28
  69.3 0.6 constant_dynamic-update-slice_fusion.27
  71.2 0.6 constant_dynamic-update-slice_fusion.24
  73.0 0.6 constant_dynamic-update-slice_fusion.21
  74.9 0.6 constant_dynamic-update-slice_fusion.18
  86.6 9.8 %all-to-all-start = ((bf16[32,1,8,16,128]{4,3,2,1,0:T(8,128)(2,1)}), bf16[32,1,8,16,128]{4,3,2,1,0:T(8,128)(2,1)S(1)}, u32[]{:S(2)}, u32[]{:S(2)}) async-start(bf16[32,1,8,16,128]{4,3,2,1,0:T(8,128)(2,1)} %constant_dynamic-update-slice_fusion), calls=%async_computation | async-start | bytes 2097152 | tf_op jit(solution)/shard_map/all_to_all | solution.py:14
  98.3 0.8 compare_reduce_fusion.4
  99.3 26.1 %all-to-all-done = bf16[32,1,8,16,128]{4,3,2,1,0:T(8,128)(2,1)S(1)} async-done(((bf16[32,1,8,16,128]{4,3,2,1,0:T(8,128)(2,1)}), bf16[32,1,8,16,128]{4,3,2,1,0:T(8,128)(2,1)S(1)}, u32[]{:S(2)}, u32[]{:S(2)}) %all-to-all-start) | async-done | bytes 1048608 | tf_op jit(solution)/shard_map/all_to_all | solution.py:14
  125.7 1.1 fusion.59
  127.1 2.6 copy.637
  129.7 2.6 copy.636
  132.3 5.8 %add_multiply_fusion = f32[8,1,8,16,128]{3,2,4,0,1:T(8,128)} fusion(f32[8,1,8,16,128]{3,2,4,0,1:T(8,128)} %copy.636, f32[8,1,8,16,128]{3,2,4,0,1:T(8,128)} %copy.637), kind=kLoop, calls=%fused_computation.7 | loop fusion | flops 262144 | bytes 1572864 | tf_op jit(solution)/shard_map/mul | solution.py:77
  138.2 2.6 copy.641
  140.8 2.4 fusion.5
  143.7 6.0 %copy.614 = f32[16,8,16,128]{2,1,3,0:T(8,128)} copy(f32[16,8,16,128]{3,2,1,0:T(8,128)} %fusion.59) | data formatting | bytes 2097152 | tf_op jit(solution)/shard_map/broadcast_in_dim | solution.py:78
  149.7 11.0 %broadcast_in_dim.122 = f32[16,2,8,16,128]{3,2,4,1,0:T(8,128)} broadcast(f32[16,8,16,128]{2,1,3,0:T(8,128)} %copy.614), dimensions={0,2,3,4} | broadcast | bytes 3145728 | tf_op jit(solution)/shard_map/broadcast_in_dim | solution.py:78
  160.7 12.0 %copy.616 = f32[32,8,16,64,2,1]{3,2,5,4,1,0:T(8,128)} copy(f32[32,8,16,64,2,1]{2,1,4,3,0,5:T(8,128)} %bitcast.344) | data formatting | bytes 4194304 | tf_op jit(solution)/shard_map/broadcast_in_dim | solution.py:78
  172.6 5.1 %copy.615 = f32[32,1,8,16,128]{0,3,4,2,1:T(8,128)} copy(bf16[32,1,8,16,128]{4,3,2,1,0:T(8,128)(2,1)S(1)} %all-to-all-done) | data formatting | bytes 3145728 | tf_op jit(solution)/shard_map/convert_element_type | solution.py:89
  177.7 8.7 %copy.617 = f32[32,8,16,64,2,1]{3,2,5,4,1,0:T(8,128)} copy(f32[32,8,16,64,2,1]{0,2,4,3,1,5:T(8,128)} %bitcast.350) | data formatting | bytes 4194304 | tf_op jit(solution)/shard_map/convert_element_type | solution.py:89
  186.4 7.6 %broadcast_in_dim.117 = f32[4,2,4,8,16,128]{4,3,5,2,1,0:T(8,128)} broadcast(f32[4,8,16,128]{2,1,3,0:T(8,128)S(1)} %fusion.5), dimensions={0,3,4,5} | broadcast | bytes 2359296 | tf_op jit(solution)/shard_map/broadcast_in_dim | solution.py:78
  194.0 11.9 %copy.619 = f32[32,8,16,64,2,1]{3,2,5,4,1,0:T(8,128)} copy(f32[32,8,16,64,2,1]{2,1,4,3,0,5:T(8,128)} %bitcast.345) | data formatting | bytes 4194304 | tf_op jit(solution)/shard_map/reshape | solution.py:78
  206.0 10.2 %broadcast_in_dim.119 = f32[8,2,2,8,16,128]{4,3,5,2,1,0:T(8,128)} broadcast(f32[8,8,16,128]{2,1,3,0:T(8,128)} %bitcast.349), dimensions={0,3,4,5} | broadcast | bytes 2621440 | tf_op jit(solution)/shard_map/broadcast_in_dim | solution.py:78
  216.2 11.9 %copy.618 = f32[32,8,16,64,2,1]{3,2,5,4,1,0:T(8,128)} copy(f32[32,8,16,64,2,1]{2,1,4,3,0,5:T(8,128)} %bitcast.346) | data formatting | bytes 4194304 | tf_op jit(solution)/shard_map/reshape | solution.py:78
  228.1 8.0 %select_select_fusion = f32[32,8,16,64,2,1]{3,2,5,4,1,0:T(8,128)S(1)} fusion(f32[32,8,16,64,2,1]{3,2,5,4,1,0:T(8,128)} %copy.619, f32[32,8,16,64,2,1]{3,2,5,4,1,0:T(8,128)} %copy.618, f32[32,8,16,64,2,1]{3,2,5,4,1,0:T(8,128)} %copy.616, f32[32,8,16,64,2,1]{3,2,5,4,1,0:T(8,128)} %copy.617, pred[16]{0:T(512)(128)(4,1)S(1)} %get-tuple-element.31, ...), kind=kLoop, calls=%fused_computation.6 | loop fusion | flops 1572864 | bytes 10485808 | tf_op jit(solution)/shard_map/jit(_where)/select_n | solution.py:96
  236.2 1.7 fusion.58
  238.3 4.5 copy.623
  242.8 4.1 broadcast_in_dim.128
  246.9 6.4 %copy.627 = bf16[32,8,16,128]{3,2,1,0:T(8,128)(2,1)} copy(bf16[32,8,16,128]{0,2,3,1:T(8,128)(2,1)} %bitcast.353) | data formatting | bytes 2097152 | tf_op jit(solution)/shard_map/broadcast_in_dim | solution.py:85
  253.3 3.6 copy.620
  256.9 2.5 fusion.1
  259.4 2.5 broadcast_in_dim.125
  261.9 6.6 %copy.628 = bf16[32,8,16,128]{3,2,1,0:T(8,128)(2,1)} copy(bf16[32,8,16,128]{0,2,3,1:T(8,128)(2,1)} %bitcast.355) | data formatting | bytes 2097152 | tf_op jit(solution)/shard_map/reshape | solution.py:85
  268.5 2.0 fusion.10
  270.5 0.9 fusion.14
  271.5 0.9 copy.656
  272.4 209.3 %reduce-scatter.4.cloned.1.call-done = bf16[8,1024]{1,0:T(8,128)(2,1)} async-done(((bf16[256,1024]{1,0:T(8,128)(2,1)}), bf16[8,1024]{1,0:T(8,128)(2,1)}) %reduce-scatter.4.cloned.1.call-update) | async-done | bytes 16400
  481.8 0.7 bitcast_convert_fusion
  482.5 0.6 copy.631
  (84 shorter events, 22.4 us)
Async XLA Ops:
  7.2 2.7 copy-start.8
  7.2 2.8 copy-start.3
  7.2 3.5 copy-start.6
  7.2 48.7 %all-gather.2.cloned.1.call-start = ((), (), s32[]{:S(2)}) async-start(), calls=%async_computation.2 | async-start | bytes 7077888 | tf_op jit(solution)/shard_map/all_gather | solution.py:108
  62.5 2.2 copy-start.1
  66.8 29.9 %copy-start.9 = (s32[512,2]{0,1:T(2,128)S(1)}, s32[512,2]{0,1:T(2,128)}, u32[]{:S(2)}) copy-start(s32[512,2]{0,1:T(2,128)} %param.11) | copy-start | bytes 12292
  69.3 27.6 %copy-start.5 = (s32[512,32]{0,1:T(8,128)S(1)}, s32[512,32]{0,1:T(8,128)}, u32[]{:S(2)}) copy-start(s32[512,32]{0,1:T(8,128)} %param.12) | copy-start | bytes 196612
  86.6 38.8 %all-to-all-start = ((bf16[32,1,8,16,128]{4,3,2,1,0:T(8,128)(2,1)}), bf16[32,1,8,16,128]{4,3,2,1,0:T(8,128)(2,1)S(1)}, u32[]{:S(2)}, u32[]{:S(2)}) async-start(bf16[32,1,8,16,128]{4,3,2,1,0:T(8,128)(2,1)} %constant_dynamic-update-slice_fusion), calls=%async_computation | async-start | bytes 2097152 | tf_op jit(solution)/shard_map/all_to_all | solution.py:14
  96.5 385.3 %reduce-scatter.4.cloned.1.call-start = ((), (), s32[]{:S(2)}) async-start(), calls=%async_computation.3 | async-start | bytes 540672
  216.2 11.9 %copy-start.7 = (pred[16]{0:T(512)(128)(4,1)S(1)}, pred[16]{0:T(512)(128)(4,1)}, u32[]{:S(2)}) copy-start(pred[16]{0:T(512)(128)(4,1)} %get-tuple-element.33) | copy-start | bytes 52
  261.9 6.6 %copy-start = (f32[16,8,16,128]{3,2,1,0:T(8,128)S(1)}, f32[16,8,16,128]{3,2,1,0:T(8,128)}, u32[]{:S(2)}) copy-start(f32[16,8,16,128]{3,2,1,0:T(8,128)} %fusion.59) | copy-start | bytes 3145732
  261.9 6.6 %copy-start.2 = (bf16[32,8,16,128]{3,2,1,0:T(8,128)(2,1)S(1)}, bf16[32,8,16,128]{3,2,1,0:T(8,128)(2,1)}, u32[]{:S(2)}) copy-start(bf16[32,8,16,128]{3,2,1,0:T(8,128)(2,1)} %copy.627) | copy-start | bytes 3145732
  270.5 1.0 copy-start.4
Sparse Core Ops, SparseCore 0:
  10.4 45.4 all-gather.1
  272.6 209.1 reduce-scatter.3
